TPU v7x, 256 devices: a whole 4x4x8 slice. The times are simulated.
256 devices in a mesh: facet: 16 (over x, y), span: 16 (over z, core).
Axes of the slice: x: 4, y: 4, z: 8, core: 2. Of those that a mesh axis runs over, the one named last changes fastest.
Arguments:
- visibilities: bfloat16 [16, 512, 2, 1024], P('span', 'facet'), may hold values from -6 to 6
- coordinates: bfloat16 [16, 512, 2, 1024], P('span', 'facet'), may hold values from 4 to 124
- phases: float32 [16, 512, 1024], P('span', 'facet'), may hold values from -3.140625 to 3.140625
- sub_index: int32 [16, 512], replicated, may hold values from 0 to 4095, as said below
Outputs:
- dirty: float32 [8192, 8192], P(('facet', 'span'))
Inputs may be any that keep to these rules, and one draw needn't show every extreme that they name: `sub_index`: within one span (one row) all 512 subgrid indices differ. A grid block is the set of subgrids with rows f * 4 to (f + 1) * 4 - 1 and columns j * 4 to (j + 1) * 4 - 1 for f < 16, j < 16; at most 4 indices of one row fall in one grid block, and in every row some grid block holds exactly 4 of them.
All inputs are finite; a program needn't handle non-finite values.
Results may differ from a plain program's by a relative error of at most 0.005.
Values may be sent and summed in bfloat16 or wider, within the bound.
No kernel may reach another device: no remote copies, remote signals or barrier semaphores. Data moves between devices by JAX's collectives and lax.ppermute only.
A program may use at most 64 MiB of HBM per device.

v0:
```python
import jax
import jax.numpy as jnp
from jax import lax
from jax.sharding import PartitionSpec as P

N = 8192
P_SIZE = 128
CAP = 4
spread = 0.75


def kernel_rows(positions, cell_index):
    gap_size = cell_index - positions[..., None]
    return jnp.exp(-(gap_size * gap_size) / (2.0 * spread * spread))


def subgrids_of(vis_items, coord_items):
    cell_index = jnp.arange(P_SIZE, dtype=jnp.float32)
    coord_vals = coord_items.astype(jnp.float32)
    row_kernel = kernel_rows(coord_vals[:, 0, :], cell_index)
    col_kernel = kernel_rows(coord_vals[:, 1, :], cell_index).astype(jnp.bfloat16)
    weighted = (vis_items.astype(jnp.float32)[:, :, :, None] * row_kernel[:, None, :, :]).astype(
        jnp.bfloat16
    )
    result = jnp.einsum("ezkp,ekq->ezpq", weighted, col_kernel, preferred_element_type=jnp.float32)
    return result.astype(jnp.bfloat16)


def group_subgrids(group_inputs):
    return subgrids_of(group_inputs[0], group_inputs[1])


def entries(sub_row, target, band_sub, col_sub, span_count):
    side_count = N // P_SIZE
    sub_rows = sub_row // side_count
    sub_cols = sub_row % side_count
    owning_block = sub_rows // band_sub * span_count + sub_cols // col_sub
    local_slot = sub_rows % band_sub * col_sub + sub_cols % col_sub
    inside = (owning_block == target).astype(jnp.int32)
    rank_of = jnp.cumsum(inside) - 1
    picked = (
        (inside[None, :] == 1) & (rank_of[None, :] == jnp.arange(CAP, dtype=jnp.int32)[:, None])
    ).astype(jnp.int32)
    block_num = jnp.arange(sub_row.shape[0], dtype=jnp.int32)
    block_ids = jnp.sum(picked * block_num[None, :], axis=1)
    slot_ids = jnp.sum(picked * local_slot[None, :], axis=1)
    filled = jnp.sum(picked, axis=1) > 0
    return (block_ids, slot_ids, filled)


def phase_table(row_count, col_count, length):
    row_ids = jnp.arange(row_count, dtype=jnp.int32)[:, None]
    col_ids = jnp.arange(col_count, dtype=jnp.int32)[None, :]
    angles = 2.0 * jnp.pi / length * (row_ids * col_ids % length).astype(jnp.float32)
    return (jnp.cos(angles), jnp.sin(angles))


def inverse_dft(real_part, imag_part):
    length = real_part.shape[-1]
    first_len = 64
    second_len = length // first_len
    leading = real_part.shape[:-1]
    split_real = real_part.reshape(leading + (first_len, second_len))
    split_imag = imag_part.reshape(leading + (first_len, second_len))
    highest = lax.Precision.HIGHEST
    cos_first, sin_first = phase_table(first_len, first_len, first_len)
    step_real = jnp.einsum(
        "av,...vb->...ab", cos_first, split_real, precision=highest
    ) - jnp.einsum("av,...vb->...ab", sin_first, split_imag, precision=highest)
    step_imag = jnp.einsum(
        "av,...vb->...ab", cos_first, split_imag, precision=highest
    ) + jnp.einsum("av,...vb->...ab", sin_first, split_real, precision=highest)
    cos_twist, sin_twist = phase_table(first_len, second_len, length)
    twist_real = step_real * cos_twist - step_imag * sin_twist
    twist_imag = step_real * sin_twist + step_imag * cos_twist
    cos_second, sin_second = phase_table(second_len, second_len, second_len)
    out_real = jnp.einsum(
        "...ab,bc->...ac", twist_real, cos_second, precision=highest
    ) - jnp.einsum("...ab,bc->...ac", twist_imag, sin_second, precision=highest)
    out_imag = jnp.einsum(
        "...ab,bc->...ac", twist_real, sin_second, precision=highest
    ) + jnp.einsum("...ab,bc->...ac", twist_imag, cos_second, precision=highest)
    out_real = jnp.swapaxes(out_real, -1, -2).reshape(leading + (length,))
    out_imag = jnp.swapaxes(out_imag, -1, -2).reshape(leading + (length,))
    return (out_real, out_imag)


def shards(visibilities, coordinates, phases, sub_index):
    facet_count = lax.axis_size("facet")
    span_count = lax.axis_size("span")
    side_count = N // P_SIZE
    band_sub = side_count // facet_count
    col_sub = side_count // span_count
    facet_id = lax.axis_index("facet")
    span_id = lax.axis_index("span")
    vis_count = visibilities.shape[3]
    vis_float = visibilities.astype(jnp.float32)
    cosine = jnp.cos(phases)
    sine = jnp.sin(phases)
    real_part = vis_float[:, :, 0, :]
    imag_part = vis_float[:, :, 1, :]
    rotated = jnp.stack(
        [real_part * cosine - imag_part * sine, real_part * sine + imag_part * cosine], axis=2
    ).astype(jnp.bfloat16)
    own_row = lax.dynamic_index_in_dim(sub_index, span_id, 0, keepdims=False)
    targets = facet_id * span_count + jnp.arange(span_count, dtype=jnp.int32)

    def send_table(target):
        return entries(own_row, target, band_sub, col_sub, span_count)

    send_ids, send_slots, send_filled = jax.vmap(send_table)(targets)
    flat_ids = send_ids.reshape(-1)
    flat_filled = send_filled.reshape(-1)
    entry_count = flat_ids.shape[0]
    blank = jnp.zeros((entry_count, 2, vis_count), jnp.bfloat16)
    pieces = (
        lax.all_gather(rotated, "facet", axis=1, tiled=True),
        lax.all_gather(coordinates, "facet", axis=1, tiled=True),
    )
    rows_here = pieces[0].shape[1]
    inside = flat_filled & (flat_ids >= 0) & (flat_ids < rows_here)
    where_row = jnp.clip(flat_ids, 0, rows_here - 1)
    vis_rows = jnp.take(pieces[0][0], where_row, axis=0)
    coord_rows = jnp.take(pieces[1][0], where_row, axis=0)
    keep_mask = inside[:, None, None]
    chosen_vis = jnp.where(keep_mask, vis_rows, blank)
    chosen_coords = jnp.where(keep_mask, coord_rows, blank)
    grouped_vis = chosen_vis.reshape(span_count, CAP, 2, vis_count)
    grouped_coords = chosen_coords.reshape(span_count, CAP, 2, vis_count)
    made_subs = lax.map(group_subgrids, (grouped_vis, grouped_coords))
    arrived = lax.all_to_all(made_subs, "span", split_axis=0, concat_axis=0, tiled=True)
    my_block = facet_id * span_count + span_id

    def recv_table(source_row):
        return entries(source_row, my_block, band_sub, col_sub, span_count)

    recv_ids, recv_slots, recv_filled = jax.vmap(recv_table)(sub_index)
    slots_here = band_sub * col_sub
    slot_range = jnp.arange(slots_here, dtype=jnp.int32)[:, None]
    onehot = (
        (recv_slots.reshape(-1)[None, :] == slot_range) & recv_filled.reshape(-1)[None, :]
    ).astype(jnp.bfloat16)
    items = arrived.reshape(span_count * CAP, 2 * P_SIZE * P_SIZE)
    summed = jnp.dot(onehot, items, preferred_element_type=jnp.float32)
    block = (
        summed.reshape(band_sub, col_sub, 2, P_SIZE, P_SIZE)
        .transpose(2, 0, 3, 1, 4)
        .reshape(2, band_sub * P_SIZE, col_sub * P_SIZE)
    )
    row_block = lax.all_to_all(block, "span", split_axis=1, concat_axis=2, tiled=True)
    half_real, half_imag = inverse_dft(row_block[0], row_block[1])
    half_done = jnp.stack([half_real, half_imag])
    columns = lax.all_to_all(
        lax.all_to_all(half_done, "facet", split_axis=2, concat_axis=1, tiled=True),
        "span",
        split_axis=2,
        concat_axis=1,
        tiled=True,
    )
    row_count = half_done.shape[1]
    col_count = columns.shape[2]
    ordered = (
        columns.reshape(2, span_count, facet_count, row_count, col_count)
        .transpose(0, 4, 2, 1, 3)
        .reshape(2, col_count, N)
    )
    image_real, image_imag = inverse_dft(ordered[0], ordered[1])
    return image_real * (1.0 / N)


def solution(mesh):
    return jax.shard_map(
        shards,
        mesh=mesh,
        in_specs=(
            P("span", "facet", None, None),
            P("span", "facet", None, None),
            P("span", "facet", None),
            P(),
        ),
        out_specs=P(("facet", "span"), None),
        check_vma=False,
    )
```

profile of v0, /device:TPU:1, one launch (start us, length us, event | category | flops | bytes accessed | tf_op | source)
XLA Modules:
  0.0 588.6 jit_solution(86421095488678001)
XLA Ops:
  12.9 49.8 %all-gather.5.cloned.1.call-done = bf16[1,512,2,1024]{3,2,0,1:T(2,128)(2,1)} async-done(((bf16[1,32,2,1024]{3,2,0,1:T(2,128)(2,1)}), bf16[1,512,2,1024]{3,2,0,1:T(2,128)(2,1)}) %all-gather.5.cloned.1.call-update) | async-done | bytes 2097168 | tf_op jit(solution)/shard_map/all_gather | solution.py:118
  62.7 2.7 gather_fusion.1
  65.4 49.1 %all-gather.3.cloned.1.call-done = bf16[1,512,2,1024]{3,2,0,1:T(2,128)(2,1)} async-done(((bf16[1,32,2,1024]{3,2,0,1:T(2,128)(2,1)}), bf16[1,512,2,1024]{3,2,0,1:T(2,128)(2,1)}) %all-gather.3.cloned.1.call-update) | async-done | bytes 2097168 | tf_op jit(solution)/shard_map/all_gather | solution.py:117
  114.6 2.7 gather_fusion
  117.9 90.2 %while.10 = (s32[]{:T(128)}, bf16[16,4,2,128,128]{4,3,2,1,0:T(8,128)(2,1)}, bf16[16,4,2,1024]{3,2,1,0:T(2,128)(2,1)S(1)}, bf16[16,4,2,1024]{3,2,1,0:T(2,128)(2,1)S(1)}, s32[]{:T(128)}) while((s32[]{:T(128)}, bf16[16,4,2,128,128]{4,3,2,1,0:T(8,128)(2,1)}, bf16[16,4,2,1024]{3,2,1,0:T(2,128)(2,1)S(1)}, bf16[16,4,2,1024]{3,2,1,0:T(2,128)(2,1)S(1)}, ...), condition=%wide.region_9.11_spmd, body=%wide.region_8.10_spmd.sunk | while | flops 275398656 | bytes 8912977 | solution.py:130
  120.5 3.1 fusion.190
  126.2 3.1 fusion.190
  131.8 3.1 fusion.190
  137.4 3.1 fusion.190
  143.1 3.1 fusion.190
  148.7 3.1 fusion.190
  154.3 3.1 fusion.190
  160.0 3.1 fusion.190
  165.6 3.1 fusion.190
  171.2 3.1 fusion.190
  176.9 3.1 fusion.190
  182.5 3.1 fusion.190
  188.1 3.1 fusion.190
  193.8 3.1 fusion.190
  199.4 3.1 fusion.190
  205.0 3.1 fusion.190
  208.1 8.5 %all-to-all-start = ((bf16[16,4,2,128,128]{4,3,2,1,0:T(8,128)(2,1)}), bf16[16,4,2,128,128]{4,3,2,1,0:T(8,128)(2,1)}, u32[]{:S(2)}, u32[]{:S(2)}) async-start(bf16[16,4,2,128,128]{4,3,2,1,0:T(8,128)(2,1)} %get-tuple-element.28), calls=%async_computation | async-start | bytes 8388608 | tf_op jit(solution)/shard_map/all_to_all | solution.py:131
  218.9 91.3 %all-to-all-done = bf16[16,4,2,128,128]{4,3,2,1,0:T(8,128)(2,1)} async-done(((bf16[16,4,2,128,128]{4,3,2,1,0:T(8,128)(2,1)}), bf16[16,4,2,128,128]{4,3,2,1,0:T(8,128)(2,1)}, u32[]{:S(2)}, u32[]{:S(2)}) %all-to-all-start) | async-done | bytes 4194336 | tf_op jit(solution)/shard_map/all_to_all | solution.py:131
  310.2 7.3 %reshape.280 = bf16[64,32768]{1,0:T(8,128)(2,1)} reshape(bf16[16,4,2,128,128]{4,3,2,1,0:T(8,128)(2,1)} %all-to-all-done) | data formatting | bytes 8388608 | tf_op jit(solution)/shard_map/reshape | solution.py:143
  317.5 3.3 copy.148
  320.9 2.6 fusion.15
  323.8 2.6 reshape.314
  326.5 5.8 all-to-all-start.1
  332.4 48.7 %all-to-all-done.1 = f32[2,512,512]{2,0,1:T(2,128)S(1)} async-done(((f32[2,512,512]{2,0,1:T(2,128)}), f32[2,512,512]{2,0,1:T(2,128)S(1)}, u32[]{:S(2)}, u32[]{:S(2)}) %all-to-all-start.1) | async-done | bytes 2097184 | tf_op jit(solution)/shard_map/all_to_all | solution.py:150
  382.5 2.1 fusion.76
  390.1 2.2 fusion.38
  393.6 2.0 copy.129
  395.5 2.3 stack_reshape.7
  397.9 3.4 fusion.23
  406.1 7.9 %copy.130 = f32[2,32,8192]{1,0,2:T(2,128)} copy(f32[2,32,8192]{2,1,0:T(8,128)S(1)} %pad_maximum_fusion) | data formatting | bytes 4194304 | tf_op jit(solution)/shard_map/stack | solution.py:152
  414.0 10.3 %reshape.317 = f32[16,1,32768]{2,1,0:T(1,128)S(1)} reshape(f32[8192,2,32]{2,1,0:T(2,128)} %bitcast.179) | data formatting | bytes 4194304
  424.3 31.8 %all_to_all.53 = f32[16,1,32768]{2,1,0:T(1,128)} all-to-all(f32[16,1,32768]{2,1,0:T(1,128)S(1)} %reshape.317), channel_id=1, replica_groups=mesh['facet'=16,'span'=16] {'facet'}, dimensions={0} | all-to-all | bytes 4194304 | tf_op jit(solution)/shard_map/all_to_all | solution.py:154
  456.6 7.3 %reduce.4 = f32[16,32768]{1,0:T(8,128)S(1)} reduce(f32[16,1,32768]{2,1,0:T(1,128)} %all_to_all.53, f32[]{:T(128)} %broadcast.473), dimensions={1}, to_apply=%all_to_all.42.reduce_sub_computation | reduce | bytes 4194308 | tf_op jit(solution)/shard_map/all_to_all | solution.py:154
  463.9 9.0 %reshape.318 = f32[8192,2,32]{2,1,0:T(2,128)} reshape(f32[16,32768]{1,0:T(8,128)S(1)} %reduce.4) | data formatting | bytes 4194304
  472.9 10.2 %copy.142 = f32[2,32,16,512]{3,1,2,0:T(8,128)S(1)} copy(f32[2,32,16,512]{1,0,3,2:T(2,128)} %bitcast.180) | data formatting | bytes 4194304 | tf_op jit(solution)/shard_map/all_to_all | solution.py:154
  483.1 2.5 copy.133
  485.6 58.1 %all_to_all.54 = f32[2,512,512]{1,0,2:T(2,128)S(1)} all-to-all(f32[2,512,512]{1,0,2:T(2,128)} %copy.133), channel_id=1, replica_groups=mesh['facet'=16,'span'=16] {'span'}, dimensions={2} | all-to-all | bytes 4194304 | tf_op jit(solution)/shard_map/all_to_all | solution.py:153
  544.0 4.4 reshape.282
  548.5 6.1 %fusion.174 = (f32[1,32,16,16,32]{4,2,1,3,0:T(8,128)S(1)}, f32[1,32,16,16,32]{4,2,1,3,0:T(8,128)}) fusion(f32[2,32,16,16,32]{4,2,1,3,0:T(8,128)} %bitcast.181), kind=kLoop, calls=%fused_computation.251 | loop fusion | bytes 4194304 | tf_op jit(solution)/shard_map/slice | solution.py:167
  554.6 4.4 copy.135
  558.9 3.3 reshape_squeeze.14
  563.4 6.5 %copy.136 = f32[1,32,16,16,32]{4,3,2,1,0:T(8,128)} copy(f32[1,32,16,16,32]{4,2,1,3,0:T(8,128)} %get-tuple-element.70) | data formatting | bytes 2097152 | tf_op jit(solution)/shard_map/slice | solution.py:167
  569.9 3.4 reshape_squeeze.15
  (171 shorter events, 73.1 us)
Async XLA Ops:
  6.5 4.0 copy-start.1
  6.5 56.2 %all-gather.5.cloned.1.call-start = ((), (), s32[]{:S(2)}) async-start(), calls=%async_computation.5 | async-start | bytes 2228224 | tf_op jit(solution)/shard_map/all_gather | solution.py:118
  7.3 107.3 %all-gather.3.cloned.1.call-start = ((), (), s32[]{:S(2)}) async-start(), calls=%async_computation.4 | async-start | bytes 2228224 | tf_op jit(solution)/shard_map/all_gather | solution.py:117
  208.1 102.1 %all-to-all-start = ((bf16[16,4,2,128,128]{4,3,2,1,0:T(8,128)(2,1)}), bf16[16,4,2,128,128]{4,3,2,1,0:T(8,128)(2,1)}, u32[]{:S(2)}, u32[]{:S(2)}) async-start(bf16[16,4,2,128,128]{4,3,2,1,0:T(8,128)(2,1)} %get-tuple-element.28), calls=%async_computation | async-start | bytes 8388608 | tf_op jit(solution)/shard_map/all_to_all | solution.py:131
  326.5 54.6 %all-to-all-start.1 = ((f32[2,512,512]{2,0,1:T(2,128)}), f32[2,512,512]{2,0,1:T(2,128)S(1)}, u32[]{:S(2)}, u32[]{:S(2)}) async-start(f32[2,512,512]{2,0,1:T(2,128)} %reshape.314), calls=%async_computation.1 | async-start | bytes 4194304 | tf_op jit(solution)/shard_map/all_to_all | solution.py:150
  385.3 1.2 copy-start
Sparse Core Ops, SparseCore 0:
  9.8 52.8 all-gather.4
  65.2 49.3 all-gather.2
where the time goes:
time: 598 us; the launch traced here: 589 us
  waiting for transfers between devices  240 us (40%)
  local copies, waits for them, and re-layouts  133 us (22%)
  blocking collectives  89.9 us (15%)
  matrix products  72.7 us (12%)
  other arithmetic  24.1 us (4%)
  starting transfers between devices  14.4 us (2%)
  between operations  14 us (2%)
    all_to_all x1, waiting for transfers between devices, shards(): lax.all_to_all(made_subs, 'span', split_axis=0, concat_axis=0, tiled=True)  91.3 us
    all_to_all x1, blocking collectives, shards(): lax.all_to_all(lax.all_to_all(half_done, 'facet', split_axis=2, concat_ax...  58.1 us
    all_gather x1, waiting for transfers between devices, shards(): lax.all_gather(coordinates, 'facet', axis=1, tiled=True)  49.8 us
    dot_general x16, matrix products, subgrids_of(): jnp.einsum('ezkp,ekq->ezpq', weighted, col_kernel, preferred_element_type...  49.2 us
    all_gather x1, waiting for transfers between devices, shards(): lax.all_gather(rotated, 'facet', axis=1, tiled=True)  49.1 us
    all_to_all x1, waiting for transfers between devices, shards(): lax.all_to_all(block, 'span', split_axis=1, concat_axis=2, tiled=True)  48.7 us
    all_to_all x1, blocking collectives, shards(): lax.all_to_all(half_done, 'facet', split_axis=2, concat_axis=1, tiled=True)  31.8 us
    exp x16, local copies, waits for them, and re-layouts, kernel_rows(): return jnp.exp(-(gap_size * gap_size) / (2.0 * spread * spread))  29.8 us
  transfers between devices with their start and end apart: 4, of which 4 were waited for; matrix products, arithmetic and copies ran while one was open for 2% of the time, Pallas kernels for 0%

commit v1 on v0

--- a/solution.py
+++ b/solution.py
@@ -1,3 +1,4 @@
+import functools
 import jax
 import jax.numpy as jnp
 from jax import lax
@@ -7,6 +8,18 @@
 P_SIZE = 128
 CAP = 4
 spread = 0.75
+
+
+def lane_fit(mine, lane_axis, out_dim, where_dim):
+    arr_next = lax.axis_size(lane_axis)
+    frame_out = jnp.split(mine, arr_next, axis=out_dim)
+    field_out = jnp.stack(frame_out)
+    carry = lax.all_to_all(field_out, lane_axis, 0, 0)
+    val2 = jnp.concatenate(carry, axis=where_dim)
+    return val2
+
+
+turn_samples_all = functools.partial(lane_fit, lane_axis="facet", out_dim=2, where_dim=1)
 
 
 def kernel_rows(positions, cell_index):
@@ -151,11 +164,7 @@
     half_real, half_imag = inverse_dft(row_block[0], row_block[1])
     half_done = jnp.stack([half_real, half_imag])
     columns = lax.all_to_all(
-        lax.all_to_all(half_done, "facet", split_axis=2, concat_axis=1, tiled=True),
-        "span",
-        split_axis=2,
-        concat_axis=1,
-        tiled=True,
+        turn_samples_all(half_done), "span", split_axis=2, concat_axis=1, tiled=True
     )
     row_count = half_done.shape[1]
     col_count = columns.shape[2]

time: 598 us -> 553 us (0.925)
  local copies, waits for them, and re-layouts: 133 us -> 97.3 us
  other arithmetic: 24.1 us -> 15.5 us
    unnamed x7 -> x21, local copies, waits for them, and re-layouts: 22.7 us -> 4.86 us
    all_to_all x4 -> x1, local copies, waits for them, and re-layouts: 13.5 us -> 0.41 us  [shards(): lax.all_to_all(turn_samples_all(half_done), 'span', split_axis=2, concat_...]
    another operation x3, local copies, waits for them, and re-layouts: 11.8 us -> 3.99 us  [shards(): half_done = jnp.stack([half_real, half_imag])]
    all_to_all x1 -> x0, other arithmetic: 7.29 us -> none  [shards(): lax.all_to_all(half_done, 'facet', split_axis=2, concat_axis=1, tiled=True)]
where the time goes in v1:
time: 553 us; the launch traced here: 544 us
  waiting for transfers between devices  240 us (43%)
  local copies, waits for them, and re-layouts  97.3 us (18%)
  blocking collectives  89.3 us (16%)
  matrix products  72.7 us (13%)
  other arithmetic  15.5 us (3%)
  starting transfers between devices  14.7 us (3%)
  between operations  14.1 us (3%)
    all_to_all x1, waiting for transfers between devices, shards(): lax.all_to_all(made_subs, 'span', split_axis=0, concat_axis=0, tiled=True)  91.3 us
    all_to_all x1, blocking collectives, shards(): lax.all_to_all(turn_samples_all(half_done), 'span', split_axis=2, concat_...  57.7 us
    all_gather x1, waiting for transfers between devices, shards(): lax.all_gather(coordinates, 'facet', axis=1, tiled=True)  49.8 us
    dot_general x16, matrix products, subgrids_of(): jnp.einsum('ezkp,ekq->ezpq', weighted, col_kernel, preferred_element_type...  49.2 us
    all_gather x1, waiting for transfers between devices, shards(): lax.all_gather(rotated, 'facet', axis=1, tiled=True)  49.1 us
    all_to_all x1, waiting for transfers between devices, shards(): lax.all_to_all(block, 'span', split_axis=1, concat_axis=2, tiled=True)  48.7 us
    all_to_all x1, blocking collectives, lane_fit(): carry = lax.all_to_all(field_out, lane_axis, 0, 0)  31.7 us
    exp x16, local copies, waits for them, and re-layouts, kernel_rows(): return jnp.exp(-(gap_size * gap_size) / (2.0 * spread * spread))  29.8 us
  transfers between devices with their start and end apart: 4, of which 4 were waited for; matrix products, arithmetic and copies ran while one was open for 2% of the time, Pallas kernels for 0%

profile of v1, /device:TPU:1, one launch (start us, length us, event | category | flops | bytes accessed | tf_op | source)
XLA Modules:
  0.0 543.8 jit_solution(13539272184350999357)
XLA Ops:
  12.9 49.8 %all-gather.5.cloned.1.call-done = bf16[1,512,2,1024]{3,2,0,1:T(2,128)(2,1)} async-done(((bf16[1,32,2,1024]{3,2,0,1:T(2,128)(2,1)}), bf16[1,512,2,1024]{3,2,0,1:T(2,128)(2,1)}) %all-gather.5.cloned.1.call-update) | async-done | bytes 2097168 | tf_op jit(solution)/shard_map/all_gather | solution.py:131
  62.7 2.7 gather_fusion.1
  65.4 49.1 %all-gather.3.cloned.1.call-done = bf16[1,512,2,1024]{3,2,0,1:T(2,128)(2,1)} async-done(((bf16[1,32,2,1024]{3,2,0,1:T(2,128)(2,1)}), bf16[1,512,2,1024]{3,2,0,1:T(2,128)(2,1)}) %all-gather.3.cloned.1.call-update) | async-done | bytes 2097168 | tf_op jit(solution)/shard_map/all_gather | solution.py:130
  114.6 2.7 gather_fusion
  117.9 90.1 %while.10 = (s32[]{:T(128)}, bf16[16,4,2,128,128]{4,3,2,1,0:T(8,128)(2,1)}, bf16[16,4,2,1024]{3,2,1,0:T(2,128)(2,1)S(1)}, bf16[16,4,2,1024]{3,2,1,0:T(2,128)(2,1)S(1)}, s32[]{:T(128)}) while((s32[]{:T(128)}, bf16[16,4,2,128,128]{4,3,2,1,0:T(8,128)(2,1)}, bf16[16,4,2,1024]{3,2,1,0:T(2,128)(2,1)S(1)}, bf16[16,4,2,1024]{3,2,1,0:T(2,128)(2,1)S(1)}, ...), condition=%wide.region_9.11_spmd, body=%wide.region_8.10_spmd.sunk | while | flops 275398656 | bytes 8912977 | solution.py:143
  118.7 1.9 copy.137
  120.5 3.1 fusion.206
  126.1 3.1 fusion.206
  129.9 1.9 copy.137
  131.8 3.1 fusion.206
  137.4 3.1 fusion.206
  141.2 1.9 copy.137
  143.0 3.1 fusion.206
  148.7 3.1 fusion.206
  152.5 1.9 copy.137
  154.3 3.1 fusion.206
  158.1 1.9 copy.137
  160.0 3.1 fusion.206
  165.6 3.1 fusion.206
  171.2 3.1 fusion.206
  176.9 3.1 fusion.206
  182.5 3.1 fusion.206
  188.1 3.1 fusion.206
  193.8 3.1 fusion.206
  199.4 3.1 fusion.206
  205.0 3.1 fusion.206
  208.1 8.5 %all-to-all-start = ((bf16[16,4,2,128,128]{4,3,2,1,0:T(8,128)(2,1)}), bf16[16,4,2,128,128]{4,3,2,1,0:T(8,128)(2,1)}, u32[]{:S(2)}, u32[]{:S(2)}) async-start(bf16[16,4,2,128,128]{4,3,2,1,0:T(8,128)(2,1)} %get-tuple-element.28), calls=%async_computation | async-start | bytes 8388608 | tf_op jit(solution)/shard_map/all_to_all | solution.py:144
  218.9 91.3 %all-to-all-done = bf16[16,4,2,128,128]{4,3,2,1,0:T(8,128)(2,1)} async-done(((bf16[16,4,2,128,128]{4,3,2,1,0:T(8,128)(2,1)}), bf16[16,4,2,128,128]{4,3,2,1,0:T(8,128)(2,1)}, u32[]{:S(2)}, u32[]{:S(2)}) %all-to-all-start) | async-done | bytes 4194336 | tf_op jit(solution)/shard_map/all_to_all | solution.py:144
  310.2 7.3 %reshape.286 = bf16[64,32768]{1,0:T(8,128)(2,1)} reshape(bf16[16,4,2,128,128]{4,3,2,1,0:T(8,128)(2,1)} %all-to-all-done) | data formatting | bytes 8388608 | tf_op jit(solution)/shard_map/reshape | solution.py:156
  317.5 3.3 copy.120
  320.9 2.6 fusion.15
  323.8 2.6 reshape.322
  326.5 6.1 %all-to-all-start.1 = ((f32[2,512,512]{2,0,1:T(2,128)}), f32[2,512,512]{2,0,1:T(2,128)S(1)}, u32[]{:S(2)}, u32[]{:S(2)}) async-start(f32[2,512,512]{2,0,1:T(2,128)} %reshape.322), calls=%async_computation.1 | async-start | bytes 4194304 | tf_op jit(solution)/shard_map/all_to_all | solution.py:163
  332.7 48.7 %all-to-all-done.1 = f32[2,512,512]{2,0,1:T(2,128)S(1)} async-done(((f32[2,512,512]{2,0,1:T(2,128)}), f32[2,512,512]{2,0,1:T(2,128)S(1)}, u32[]{:S(2)}, u32[]{:S(2)}) %all-to-all-start.1) | async-done | bytes 2097184 | tf_op jit(solution)/shard_map/all_to_all | solution.py:163
  382.8 2.1 fusion.92
  390.4 2.2 fusion.38
  393.9 2.0 copy.105
  395.8 2.3 stack_reshape.7
  398.1 3.4 fusion.23
  406.7 31.7 %all_to_all.40 = f32[16,2,32,512]{3,2,1,0:T(8,128)S(1)} all-to-all(f32[16,2,32,512]{3,2,1,0:T(8,128)S(1)} %fusion.39), channel_id=1, replica_groups=mesh['facet'=16,'span'=16] {'facet'}, dimensions={0} | all-to-all | bytes 4194304 | tf_op jit(solution)/shard_map/all_to_all | solution.py:17
  438.6 2.5 copy.107
  441.1 57.7 %all_to_all.41 = f32[2,512,512]{1,0,2:T(2,128)S(1)} all-to-all(f32[2,512,512]{1,0,2:T(2,128)} %copy.107), channel_id=1, replica_groups=mesh['facet'=16,'span'=16] {'span'}, dimensions={2} | all-to-all | bytes 4194304 | tf_op jit(solution)/shard_map/all_to_all | solution.py:166
  499.2 4.4 reshape.290
  503.6 6.1 %fusion.190 = (f32[1,32,16,16,32]{4,2,1,3,0:T(8,128)S(1)}, f32[1,32,16,16,32]{4,2,1,3,0:T(8,128)}) fusion(f32[2,32,16,16,32]{4,2,1,3,0:T(8,128)} %bitcast.238), kind=kLoop, calls=%fused_computation.284 | loop fusion | bytes 4194304 | tf_op jit(solution)/shard_map/slice | solution.py:176
  509.7 4.4 copy.109
  514.0 3.3 reshape_squeeze.14
  518.5 6.5 %copy.110 = f32[1,32,16,16,32]{4,3,2,1,0:T(8,128)} copy(f32[1,32,16,16,32]{4,2,1,3,0:T(8,128)} %get-tuple-element.66) | data formatting | bytes 2097152 | tf_op jit(solution)/shard_map/slice | solution.py:176
  525.0 3.5 reshape_squeeze.15
  (183 shorter events, 63.8 us)
Async XLA Ops:
  6.5 4.0 copy-start.1
  6.5 56.2 %all-gather.5.cloned.1.call-start = ((), (), s32[]{:S(2)}) async-start(), calls=%async_computation.5 | async-start | bytes 2228224 | tf_op jit(solution)/shard_map/all_gather | solution.py:131
  7.3 107.3 %all-gather.3.cloned.1.call-start = ((), (), s32[]{:S(2)}) async-start(), calls=%async_computation.4 | async-start | bytes 2228224 | tf_op jit(solution)/shard_map/all_gather | solution.py:130
  208.1 102.1 %all-to-all-start = ((bf16[16,4,2,128,128]{4,3,2,1,0:T(8,128)(2,1)}), bf16[16,4,2,128,128]{4,3,2,1,0:T(8,128)(2,1)}, u32[]{:S(2)}, u32[]{:S(2)}) async-start(bf16[16,4,2,128,128]{4,3,2,1,0:T(8,128)(2,1)} %get-tuple-element.28), calls=%async_computation | async-start | bytes 8388608 | tf_op jit(solution)/shard_map/all_to_all | solution.py:144
  326.5 54.9 %all-to-all-start.1 = ((f32[2,512,512]{2,0,1:T(2,128)}), f32[2,512,512]{2,0,1:T(2,128)S(1)}, u32[]{:S(2)}, u32[]{:S(2)}) async-start(f32[2,512,512]{2,0,1:T(2,128)} %reshape.322), calls=%async_computation.1 | async-start | bytes 4194304 | tf_op jit(solution)/shard_map/all_to_all | solution.py:163
  385.6 1.2 copy-start
Sparse Core Ops, SparseCore 0:
  9.8 52.8 all-gather.4
  65.2 49.3 all-gather.2
